TPU v7x, 32 devices: a whole 2x2x4 slice. The times are simulated.
32 devices in a mesh: dp: 8 (over z, y), mp: 4 (over x, core).
Axes of the slice: x: 2, y: 2, z: 4, core: 2. Of those that a mesh axis runs over, the one named last changes fastest.
Arguments:
- tokens: bfloat16 [32, 256, 1152], P('dp'), may hold values from -6 to 6
- condition: bfloat16 [32, 1152], P('dp'), may hold values from -6 to 6
- cotangent: bfloat16 [32, 256, 1152], P('dp'), may hold values from -12 to 12
- kept_index: int32 [32, 128], P('dp'), may hold values from 0 to 255, as said below
- skip_index: int32 [32, 128], P('dp'), may hold values from 0 to 255, as said below
- step_count: int32 [1], replicated, may hold values from 1 to 20
- ada_weight: float32 [1152, 6, 1152], P('dp', None, 'mp'), may hold values from -0.1875 to 0.1875
- qkv_weight: float32 [3, 1152, 1152], P(None, 'dp', 'mp'), may hold values from -0.1875 to 0.1875
- proj_weight: float32 [1152, 1152], P('mp', 'dp'), may hold values from -1 to 1
- fc1_weight: float32 [1152, 4608], P('dp', 'mp'), may hold values from -0.1875 to 0.1875
- fc2_weight: float32 [4608, 1152], P('mp', 'dp'), may hold values from -0.09375 to 0.09375
- ada_moment: float32 [1152, 6, 1152], P('dp', None, 'mp'), may hold values from -80 to 80
- qkv_moment: float32 [3, 1152, 1152], P(None, 'dp', 'mp'), may hold values from -80 to 80
- proj_moment: float32 [1152, 1152], P('mp', 'dp'), may hold values from -80 to 80
- fc1_moment: float32 [1152, 4608], P('dp', 'mp'), may hold values from -80 to 80
- fc2_moment: float32 [4608, 1152], P('mp', 'dp'), may hold values from -80 to 80
- ada_average: float32 [1152, 6, 1152], P('dp', None, 'mp'), may hold values from -0.1875 to 0.1875
- qkv_average: float32 [3, 1152, 1152], P(None, 'dp', 'mp'), may hold values from -0.1875 to 0.1875
- proj_average: float32 [1152, 1152], P('mp', 'dp'), may hold values from -1 to 1
- fc1_average: float32 [1152, 4608], P('dp', 'mp'), may hold values from -0.1875 to 0.1875
- fc2_average: float32 [4608, 1152], P('mp', 'dp'), may hold values from -0.09375 to 0.09375
Outputs:
- block_out: bfloat16 [32, 256, 1152], P('dp')
- tokens_grad: float32 [32, 256, 1152], P('dp')
- condition_grad: float32 [32, 1152], P('dp')
- ada_master: float32 [1152, 6, 1152], P('dp', None, 'mp')
- qkv_master: float32 [3, 1152, 1152], P(None, 'dp', 'mp')
- proj_master: float32 [1152, 1152], P('mp', 'dp')
- fc1_master: float32 [1152, 4608], P('dp', 'mp')
- fc2_master: float32 [4608, 1152], P('mp', 'dp')
- ada_momentum: float32 [1152, 6, 1152], P('dp', None, 'mp')
- qkv_momentum: float32 [3, 1152, 1152], P(None, 'dp', 'mp')
- proj_momentum: float32 [1152, 1152], P('mp', 'dp')
- fc1_momentum: float32 [1152, 4608], P('dp', 'mp')
- fc2_momentum: float32 [4608, 1152], P('mp', 'dp')
- ada_ema: float32 [1152, 6, 1152], P('dp', None, 'mp')
- qkv_ema: float32 [3, 1152, 1152], P(None, 'dp', 'mp')
- proj_ema: float32 [1152, 1152], P('mp', 'dp')
- fc1_ema: float32 [1152, 4608], P('dp', 'mp')
- fc2_ema: float32 [4608, 1152], P('mp', 'dp')
Inputs may be any that keep to these rules, and one draw needn't show every extreme that they name: `kept_index`: row b lists 128 distinct positions of image b in increasing order; row b of skip_index lists the other 128 positions in increasing order. `skip_index`: row b lists the positions of image b that kept_index does not, in increasing order.
All inputs are finite; a program needn't handle non-finite values.
Results may differ from a plain program's by a relative error of at most 0.012.
The roundings to bfloat16 on the way count: a program that leaves them out, or rounds other values in their place, can miss the bound.
Values may be sent and summed in bfloat16 or wider, within the bound.
No kernel may reach another device: no remote copies, remote signals or barrier semaphores. Data moves between devices by JAX's collectives and lax.ppermute only.
A program may use at most 192 MiB of HBM per device.

v0:
```python
from functools import partial
import math
import jax
import jax.numpy as jnp
from jax import lax
from jax.sharding import PartitionSpec as P

HEAD_DIM = 72
epsilon = 1e-06
momentum_rate = 0.9


def layer_norm(values):
    centered = values - jnp.mean(values, axis=-1, keepdims=True)
    inverse = lax.rsqrt(jnp.mean(centered * centered, axis=-1, keepdims=True) + epsilon)
    return (centered * inverse, inverse)


def norm_back(normed, inverse, gradient):
    return inverse * (
        gradient
        - jnp.mean(gradient, axis=-1, keepdims=True)
        - normed * jnp.mean(gradient * normed, axis=-1, keepdims=True)
    )


def pick_rows(values, index):
    return jnp.take_along_axis(values, index[:, :, None], axis=1)


def place_rows(kept_rows, other_rows, kept_index, skip_index):
    images = kept_index.shape[0]
    batch = jnp.arange(images, dtype=jnp.int32)[:, None]
    blank = jnp.zeros(
        (images, kept_index.shape[1] + skip_index.shape[1], kept_rows.shape[2]), kept_rows.dtype
    )
    return blank.at[batch, kept_index].set(kept_rows).at[batch, skip_index].set(other_rows)


def share_rows(values):
    return lax.psum_scatter(values, "mp", scatter_dimension=1, tiled=True)


def whole_rows(values):
    return lax.all_gather(values, "mp", axis=1, tiled=True)


def per_device(
    tokens,
    condition,
    cotangent,
    kept_index,
    skip_index,
    step_count,
    ada_weight,
    qkv_weight,
    proj_weight,
    fc1_weight,
    fc2_weight,
    ada_moment,
    qkv_moment,
    proj_moment,
    fc1_moment,
    fc2_moment,
    ada_average,
    qkv_average,
    proj_average,
    fc1_average,
    fc2_average,
):
    f32 = jnp.float32
    bf16 = jnp.bfloat16
    ada_low = ada_weight.astype(bf16)
    qkv_low = qkv_weight.astype(bf16)
    proj_low = proj_weight.astype(bf16)
    fc1_low = fc1_weight.astype(bf16)
    fc2_low = fc2_weight.astype(bf16)
    ada_full, qkv_full, proj_full, fc1_full, fc2_full = (
        lax.all_gather(ada_low, "dp", axis=0, tiled=True),
        lax.all_gather(qkv_low, "dp", axis=1, tiled=True),
        lax.all_gather(proj_low, "dp", axis=1, tiled=True),
        lax.all_gather(fc1_low, "dp", axis=0, tiled=True),
        lax.all_gather(fc2_low, "dp", axis=1, tiled=True),
    )
    images = tokens.shape[0]
    kept_count = kept_index.shape[1]
    local_width = qkv_full.shape[2]
    local_heads = local_width // HEAD_DIM
    score_scale = HEAD_DIM ** (-0.5)
    row_share = kept_count // lax.axis_size("mp")
    row_start = lax.axis_index("mp") * row_share

    def own_rows(values):
        return lax.dynamic_slice_in_dim(values, row_start, row_share, 1)

    cond_float = condition.astype(f32)
    silu_cond = jax.nn.silu(cond_float).astype(bf16)
    mod_part = jnp.einsum("bd,dkf->bkf", silu_cond, ada_full, preferred_element_type=f32)
    modulation = lax.all_gather(mod_part, "mp", axis=2, tiled=True)
    shift_one = modulation[:, 0, None, :]
    scale_one = modulation[:, 1, None, :]
    gate_one = modulation[:, 2, None, :]
    shift_two = modulation[:, 3, None, :]
    scale_two = modulation[:, 4, None, :]
    gate_two = modulation[:, 5, None, :]
    kept_rows = pick_rows(tokens, kept_index).astype(f32)
    normed_one, inverse_one = layer_norm(kept_rows)
    hidden = (normed_one * (1.0 + scale_one) + shift_one).astype(bf16)
    projected = jnp.einsum("bnd,tdf->tbnf", hidden, qkv_full, preferred_element_type=f32).astype(
        bf16
    )
    split_heads = projected.reshape(3, images, kept_count, local_heads, HEAD_DIM)
    query_heads = split_heads[0]
    key_heads = split_heads[1]
    value_heads = split_heads[2]
    scores = (
        jnp.einsum("bqhe,bkhe->bhqk", query_heads, key_heads, preferred_element_type=f32)
        * score_scale
    )
    row_max = jnp.max(scores, axis=-1, keepdims=True)
    exp_scores = jnp.exp(scores - row_max)
    row_total = jnp.sum(exp_scores, axis=-1, keepdims=True)
    log_total = row_max + jnp.log(row_total)
    probs = exp_scores / row_total
    attended = (
        jnp.einsum("bhqk,bkhe->bqhe", probs.astype(bf16), value_heads, preferred_element_type=f32)
        .astype(bf16)
        .reshape(images, kept_count, local_width)
    )
    attn_part = jnp.einsum("bnf,fd->bnd", attended, proj_full, preferred_element_type=f32)
    attn_out = share_rows(attn_part)
    residual = own_rows(kept_rows) + gate_one * attn_out
    normed_two, inverse_two = layer_norm(residual)
    hidden_two = whole_rows((normed_two * (1.0 + scale_two) + shift_two).astype(bf16))
    pre_act = jnp.einsum("bnd,df->bnf", hidden_two, fc1_full, preferred_element_type=f32)
    activated = jax.nn.gelu(pre_act, approximate=True).astype(bf16)
    mlp_part = jnp.einsum("bnf,fd->bnd", activated, fc2_full, preferred_element_type=f32)
    mlp_out = share_rows(mlp_part)
    kept_out = residual + gate_two * mlp_out
    kept_low = whole_rows(kept_out.astype(bf16))
    block_out = place_rows(kept_low, pick_rows(tokens, skip_index), kept_index, skip_index)
    ada_back, qkv_back, proj_back, fc1_back, fc2_back = (
        lax.all_gather(ada_low, "dp", axis=0, tiled=True),
        lax.all_gather(qkv_low, "dp", axis=1, tiled=True),
        lax.all_gather(proj_low, "dp", axis=1, tiled=True),
        lax.all_gather(fc1_low, "dp", axis=0, tiled=True),
        lax.all_gather(fc2_low, "dp", axis=1, tiled=True),
    )
    grad_float = cotangent.astype(f32)
    grad_kept = pick_rows(grad_float, kept_index)
    grad_here = own_rows(grad_kept)
    gate_two_grad = jnp.sum(grad_here * mlp_out, axis=1)
    mlp_out_grad = (gate_two * grad_kept).astype(bf16)
    fc2_grad = jnp.einsum("bnf,bnd->fd", activated, mlp_out_grad, preferred_element_type=f32)
    act_grad = jnp.einsum("bnd,fd->bnf", mlp_out_grad, fc2_back, preferred_element_type=f32)
    gelu_value, gelu_pull = jax.vjp(partial(jax.nn.gelu, approximate=True), pre_act)
    pre_grad = gelu_pull(act_grad)[0].astype(bf16)
    fc1_grad = jnp.einsum("bnd,bnf->df", hidden_two, pre_grad, preferred_element_type=f32)
    hidden_two_part = jnp.einsum("bnf,df->bnd", pre_grad, fc1_back, preferred_element_type=f32)
    hidden_two_grad = share_rows(hidden_two_part)
    shift_two_grad = jnp.sum(hidden_two_grad, axis=1)
    scale_two_grad = jnp.sum(hidden_two_grad * normed_two, axis=1)
    residual_grad = grad_here + norm_back(
        normed_two, inverse_two, hidden_two_grad * (1.0 + scale_two)
    )
    gate_one_grad = jnp.sum(residual_grad * attn_out, axis=1)
    attn_out_grad = whole_rows((gate_one * residual_grad).astype(bf16))
    proj_grad = jnp.einsum("bnf,bnd->fd", attended, attn_out_grad, preferred_element_type=f32)
    attended_grad = jnp.einsum(
        "bnd,fd->bnf", attn_out_grad, proj_back, preferred_element_type=f32
    ).astype(bf16)
    attended_grad = attended_grad.reshape(images, kept_count, local_heads, HEAD_DIM)
    again_scores = (
        jnp.einsum("bqhe,bkhe->bhqk", query_heads, key_heads, preferred_element_type=f32)
        * score_scale
    )
    again_probs = jnp.exp(again_scores - log_total)
    prob_grad = jnp.einsum(
        "bqhe,bkhe->bhqk", attended_grad, value_heads, preferred_element_type=f32
    )
    score_grad = (
        again_probs * (prob_grad - jnp.sum(prob_grad * again_probs, axis=-1, keepdims=True))
    ).astype(bf16)
    query_grad = (
        jnp.einsum("bhqk,bkhe->bqhe", score_grad, key_heads, preferred_element_type=f32)
        * score_scale
    )
    key_grad = (
        jnp.einsum("bhqk,bqhe->bkhe", score_grad, query_heads, preferred_element_type=f32)
        * score_scale
    )
    value_grad = jnp.einsum(
        "bhqk,bqhe->bkhe", again_probs.astype(bf16), attended_grad, preferred_element_type=f32
    )
    grad_rows = (
        jnp.stack([query_grad, key_grad, value_grad])
        .astype(bf16)
        .reshape(3, images, kept_count, local_width)
    )
    qkv_grad = jnp.einsum("tbnf,bnd->tdf", grad_rows, hidden, preferred_element_type=f32)
    hidden_part = jnp.einsum("tbnf,tdf->bnd", grad_rows, qkv_back, preferred_element_type=f32)
    hidden_grad = share_rows(hidden_part)
    normed_here = own_rows(normed_one)
    inverse_here = own_rows(inverse_one)
    shift_one_grad = jnp.sum(hidden_grad, axis=1)
    scale_one_grad = jnp.sum(hidden_grad * normed_here, axis=1)
    kept_share = residual_grad + norm_back(
        normed_here, inverse_here, hidden_grad * (1.0 + scale_one)
    )
    kept_grad = lax.all_gather(kept_share, "mp", axis=1, tiled=True)
    tokens_grad = place_rows(kept_grad, pick_rows(grad_float, skip_index), kept_index, skip_index)
    mod_grad = jnp.stack(
        [
            shift_one_grad,
            scale_one_grad,
            gate_one_grad,
            shift_two_grad,
            scale_two_grad,
            gate_two_grad,
        ],
        axis=1,
    )
    mod_local = lax.psum_scatter(mod_grad, "mp", scatter_dimension=2, tiled=True).astype(bf16)
    ada_grad = jnp.einsum("bd,bkf->dkf", silu_cond, mod_local, preferred_element_type=f32)
    silu_grad = lax.psum(
        jnp.einsum("bkf,dkf->bd", mod_local, ada_back, preferred_element_type=f32), "mp"
    )
    silu_value, silu_pull = jax.vjp(jax.nn.silu, cond_float)
    condition_grad = silu_pull(silu_grad)[0]
    ada_shard, qkv_shard, proj_shard, fc1_shard, fc2_shard = (
        lax.psum_scatter(ada_grad, "dp", scatter_dimension=0, tiled=True),
        lax.psum_scatter(qkv_grad, "dp", scatter_dimension=1, tiled=True),
        lax.psum_scatter(proj_grad, "dp", scatter_dimension=1, tiled=True),
        lax.psum_scatter(fc1_grad, "dp", scatter_dimension=0, tiled=True),
        lax.psum_scatter(fc2_grad, "dp", scatter_dimension=1, tiled=True),
    )
    rate = 0.02 / math.sqrt(images * lax.axis_size("dp") * kept_count)
    step_float = step_count.astype(f32)[0]
    decay = (1.0 + step_float) / (10.0 + step_float)

    def update(weight, moment, average, gradient):
        new_moment = momentum_rate * moment + gradient
        master = weight - rate * (gradient + momentum_rate * new_moment)
        return (master, new_moment, decay * average + (1.0 - decay) * master)

    ada_master, ada_momentum, ada_ema = update(ada_weight, ada_moment, ada_average, ada_shard)
    qkv_master, qkv_momentum, qkv_ema = update(qkv_weight, qkv_moment, qkv_average, qkv_shard)
    proj_master, proj_momentum, proj_ema = update(
        proj_weight, proj_moment, proj_average, proj_shard
    )
    fc1_master, fc1_momentum, fc1_ema = update(fc1_weight, fc1_moment, fc1_average, fc1_shard)
    fc2_master, fc2_momentum, fc2_ema = update(fc2_weight, fc2_moment, fc2_average, fc2_shard)
    return (
        block_out,
        tokens_grad,
        condition_grad,
        ada_master,
        qkv_master,
        proj_master,
        fc1_master,
        fc2_master,
        ada_momentum,
        qkv_momentum,
        proj_momentum,
        fc1_momentum,
        fc2_momentum,
        ada_ema,
        qkv_ema,
        proj_ema,
        fc1_ema,
        fc2_ema,
    )


def solution(mesh):
    placed = (
        P("dp", None, None),
        P("dp", None),
        P("dp", None, None),
        P("dp", None),
        P("dp", None),
        P(),
        P("dp", None, "mp"),
        P(None, "dp", "mp"),
        P("mp", "dp"),
        P("dp", "mp"),
        P("mp", "dp"),
        P("dp", None, "mp"),
        P(None, "dp", "mp"),
        P("mp", "dp"),
        P("dp", "mp"),
        P("mp", "dp"),
        P("dp", None, "mp"),
        P(None, "dp", "mp"),
        P("mp", "dp"),
        P("dp", "mp"),
        P("mp", "dp"),
    )
    return jax.shard_map(
        per_device,
        mesh=mesh,
        in_specs=placed,
        out_specs=(
            P("dp", None, None),
            P("dp", None, None),
            P("dp", None),
            P("dp", None, "mp"),
            P(None, "dp", "mp"),
            P("mp", "dp"),
            P("dp", "mp"),
            P("mp", "dp"),
            P("dp", None, "mp"),
            P(None, "dp", "mp"),
            P("mp", "dp"),
            P("dp", "mp"),
            P("mp", "dp"),
            P("dp", None, "mp"),
            P(None, "dp", "mp"),
            P("mp", "dp"),
            P("dp", "mp"),
            P("mp", "dp"),
        ),
        check_vma=False,
    )
```

profile of v0, /device:TPU:0, one launch (start us, length us, event | category | flops | bytes accessed | tf_op | source)
XLA Modules:
  0.0 1142.5 jit_solution(12994166128726137092)
XLA Ops:
  7.3 2.4 convert_element_type.83
  11.3 5.7 gather_fusion
  18.1 38.6 %all_gather.38 = bf16[288,1152]{0,1:T(8,128)(2,1)} all-gather(bf16[288,144]{0,1:T(8,128)(2,1)S(1)} %copy-done.21), channel_id=1, replica_groups=mesh['dp'=8,'mp'=4] {'dp'}, dimensions={1}, use_global_device_ids=true | all-gather | bytes 746496 | tf_op jit(solution)/shard_map/all_gather | solution.py:81
  56.7 51.9 %all-gather.9.cloned.1.call-done = bf16[1152,6,288]{2,0,1:T(8,128)(2,1)} async-done(((bf16[144,6,288]{2,0,1:T(8,128)(2,1)}), bf16[1152,6,288]{2,0,1:T(8,128)(2,1)}) %all-gather.9.cloned.1.call-update) | async-done | bytes 3981328 | tf_op jit(solution)/shard_map/all_gather | solution.py:79
  108.6 3.9 fusion.50
  114.4 17.3 %all_gather.36 = f32[4,6,1152]{1,0,2:T(4,128)S(1)} all-gather(f32[4,6,288]{1,0,2:T(4,128)} %copy.115), channel_id=1, replica_groups=mesh['dp'=8,'mp'=4] {'mp'}, dimensions={2}, use_global_device_ids=true | all-gather | bytes 138240 | tf_op jit(solution)/shard_map/all_gather | solution.py:99
  131.7 9.2 fusion.74
  140.9 2.7 copy.149
  143.6 2.7 copy.118
  147.7 17.1 %all-gather.11.cloned.1.call-done = bf16[3,1152,288]{2,1,0:T(8,128)(2,1)} async-done(((bf16[3,144,288]{2,1,0:T(8,128)(2,1)}), bf16[3,1152,288]{2,1,0:T(8,128)(2,1)}) %all-gather.11.cloned.1.call-update) | async-done | bytes 1990672 | tf_op jit(solution)/shard_map/all_gather | solution.py:80
  164.7 3.6 fusion.23
  176.6 2.8 copy.116
  179.3 2.8 copy.150
  182.2 2.7 copy.122
  186.2 18.3 %reduce-scatter.15.cloned.1.call-done = f32[4,32,1152]{2,1,0:T(8,128)} async-done(((f32[4,128,1152]{2,1,0:T(8,128)}), f32[4,32,1152]{2,1,0:T(8,128)}) %reduce-scatter.15.cloned.1.call-update) | async-done | bytes 589840 | tf_op jit(solution)/shard_map/reduce_scatter | solution.py:41
  207.8 4.2 convert_element_type.97
  212.0 11.0 gather_fusion.2
  222.9 4.3 subtract_multiply_fusion
  227.2 2.7 copy.120
  230.0 32.5 %all-gather.15.cloned.1.call-done = bf16[1152,1152]{1,0:T(8,128)(2,1)} async-done(((bf16[144,1152]{1,0:T(8,128)(2,1)}), bf16[1152,1152]{1,0:T(8,128)(2,1)}) %all-gather.15.cloned.1.call-update) | async-done | bytes 2654224 | tf_op jit(solution)/shard_map/all_gather | solution.py:82
  262.5 18.1 %all-gather.13.cloned.1.call-done = bf16[4,128,1152]{2,1,0:T(8,128)(2,1)} async-done(((bf16[4,32,1152]{2,1,0:T(8,128)(2,1)}), bf16[4,128,1152]{2,1,0:T(8,128)(2,1)}) %all-gather.13.cloned.1.call-update) | async-done | bytes 1179664 | tf_op jit(solution)/shard_map/all_gather | solution.py:45
  280.6 4.1 fusion.6
  286.1 4.3 convolution_bitcast_fusion
  291.1 103.6 %reduce-scatter.29.cloned.1.call-done = f32[1152,144]{0,1:T(8,128)} async-done(((f32[1152,1152]{0,1:T(8,128)}), f32[1152,144]{0,1:T(8,128)}) %reduce-scatter.29.cloned.1.call-update) | async-done | bytes 663568 | tf_op jit(solution)/shard_map/reduce_scatter | solution.py:235
  394.7 3.4 multiply_add_fusion.4
  398.2 54.9 %all-gather.17.cloned.1.call-done = bf16[1152,1152]{0,1:T(8,128)(2,1)} async-done(((bf16[1152,144]{0,1:T(8,128)(2,1)}), bf16[1152,1152]{0,1:T(8,128)(2,1)}) %all-gather.17.cloned.1.call-update) | async-done | bytes 2654224 | tf_op jit(solution)/shard_map/all_gather | solution.py:83
  453.1 5.8 fusion.17
  459.9 3.4 fusion.4
  463.6 6.1 fusion.2
  469.7 25.4 %reduce-scatter.19.cloned.1.call-done = f32[4,32,1152]{2,1,0:T(8,128)} async-done(((f32[4,128,1152]{2,1,0:T(8,128)}), f32[4,32,1152]{2,1,0:T(8,128)}) %reduce-scatter.19.cloned.1.call-update) | async-done | bytes 589840 | tf_op jit(solution)/shard_map/reduce_scatter | solution.py:41
  497.9 33.0 %reduce-scatter.17.cloned.1.call-done = f32[4,32,1152]{2,1,0:T(8,128)} async-done(((f32[4,128,1152]{2,1,0:T(8,128)}), f32[4,32,1152]{2,1,0:T(8,128)}) %reduce-scatter.17.cloned.1.call-update) | async-done | bytes 589840 | tf_op jit(solution)/shard_map/reduce_scatter | solution.py:41
  531.0 3.5 multiply_reduce_fusion.4
  536.8 16.8 %all-gather.21.cloned.1.call-done = bf16[4,128,1152]{2,1,0:T(8,128)(2,1)} async-done(((bf16[4,32,1152]{2,1,0:T(8,128)(2,1)}), bf16[4,128,1152]{2,1,0:T(8,128)(2,1)}) %all-gather.21.cloned.1.call-update) | async-done | bytes 1179664 | tf_op jit(solution)/shard_map/all_gather | solution.py:45
  559.0 3.4 convolution_bitcast_fusion.3
  562.4 33.2 %reduce-scatter.21.cloned.1.call-done = f32[4,32,1152]{2,1,0:T(8,128)} async-done(((f32[4,128,1152]{2,1,0:T(8,128)}), f32[4,32,1152]{2,1,0:T(8,128)}) %reduce-scatter.21.cloned.1.call-update) | async-done | bytes 589840 | tf_op jit(solution)/shard_map/reduce_scatter | solution.py:41
  604.3 3.8 copy.145
  608.0 4.1 reshape.212
  613.0 3.4 convolution_bitcast_fusion.4
  616.5 5.8 convolution_bitcast_fusion.1
  622.9 4.7 convolution_bitcast_fusion.2
  627.6 8.6 copy.147
  636.2 9.0 reshape.214
  651.3 5.7 fusion.46
  658.4 11.0 gather_fusion.3
  669.4 8.4 gather_fusion.1
  677.7 2.4 copy.130
  682.5 2.7 broadcast_select_fusion.2
  688.4 78.5 %scatter_fusion = bf16[4,256,1152]{2,1,0:T(8,128)(2,1)} fusion(bf16[4,256,1152]{2,1,0:T(8,128)(2,1)} %broadcast_in_dim.28, s32[512]{0:T(512)S(1)} %get-tuple-element.152, bf16[512,1152]{1,0:T(8,128)(2,1)} %bitcast.198), kind=kCustom, calls=%fused_computation.4 | custom fusion | bytes 3543040 | tf_op jit(solution)/shard_map/scatter | solution.py:37
  766.9 78.8 %scatter_fusion.1 = bf16[4,256,1152]{2,1,0:T(8,128)(2,1)} fusion(bf16[4,256,1152]{2,1,0:T(8,128)(2,1)} %scatter_fusion, s32[512]{0:T(512)S(1)} %get-tuple-element.150, bf16[512,1152]{1,0:T(8,128)(2,1)} %bitcast.187), kind=kCustom, calls=%fused_computation.5 | custom fusion | bytes 3543040 | tf_op jit(solution)/shard_map/scatter | solution.py:37
  847.7 3.2 multiply_add_fusion.5
  850.9 4.0 convolution_bitcast_fusion.5
  854.9 11.2 psum.7
  866.8 55.1 %reduce-scatter.33.cloned.1.call-done = f32[144,864]{1,0:T(8,128)} async-done(((f32[1152,864]{1,0:T(8,128)}), f32[144,864]{1,0:T(8,128)}) %reduce-scatter.33.cloned.1.call-update) | async-done | bytes 497680
  921.9 2.4 reshape.215
  924.3 2.4 copy.148
  926.7 3.5 multiply_add_fusion.2
  930.2 2.5 copy.134
  932.8 2.3 copy.135
  936.3 10.9 all-gather.23.cloned.1.call-done
  947.2 2.5 broadcast_in_dim.35
  949.7 80.0 %scatter_fusion.2 = f32[4,256,1152]{2,1,0:T(8,128)} fusion(f32[4,256,1152]{2,1,0:T(8,128)} %broadcast_in_dim.35, s32[512]{0:T(512)S(1)} %get-tuple-element.152, f32[512,1152]{1,0:T(8,128)} %bitcast.196), kind=kCustom, calls=%fused_computation.6 | custom fusion | bytes 7081984 | tf_op jit(solution)/shard_map/scatter | solution.py:37
  1029.7 79.8 %scatter_fusion.3 = f32[4,256,1152]{2,1,0:T(8,128)} fusion(f32[4,256,1152]{2,1,0:T(8,128)} %scatter_fusion.2, s32[512]{0:T(512)S(1)} %get-tuple-element.150, f32[512,1152]{1,0:T(8,128)} %bitcast.184), kind=kCustom, calls=%fused_computation.7 | custom fusion | bytes 7081984 | tf_op jit(solution)/shard_map/scatter | solution.py:37
  1109.5 21.1 %reduce-scatter.23.cloned.1.call-done = f32[144,6,288]{2,0,1:T(8,128)} async-done(((f32[1152,6,288]{2,0,1:T(8,128)}), f32[144,6,288]{2,0,1:T(8,128)}) %reduce-scatter.23.cloned.1.call-update) | async-done | bytes 995344 | tf_op jit(solution)/shard_map/reduce_scatter | solution.py:231
  1130.6 4.8 multiply_add_fusion
  (185 shorter events, 58.9 us)
Async XLA Ops:
  7.2 4.1 copy-start
  7.2 2.5 copy-start.14
  7.2 3.4 copy-start.19
  7.2 4.0 copy-start.39
  7.2 101.4 %all-gather.9.cloned.1.call-start = ((), (), s32[]{:S(2)}) async-start(), calls=%async_computation.10 | async-start | bytes 5971968 | tf_op jit(solution)/shard_map/all_gather | solution.py:79
  9.7 155.0 %all-gather.11.cloned.1.call-start = ((), (), s32[]{:S(2)}) async-start(), calls=%async_computation.11 | async-start | bytes 2985984 | tf_op jit(solution)/shard_map/all_gather | solution.py:80
  10.5 194.0 %reduce-scatter.15.cloned.1.call-start = ((), (), s32[]{:S(2)}) async-start(), calls=%async_computation.12 | async-start | bytes 2949120 | tf_op jit(solution)/shard_map/reduce_scatter | solution.py:41
  17.0 1.1 copy-start.21
  17.0 0.5 copy-start.36
  17.5 147.2 %copy-start.32 = (f32[4,128]{1,0:T(4,128)}, f32[4,128]{1,0:T(4,128)S(1)}, u32[]{:S(2)}) copy-start(f32[4,128]{1,0:T(4,128)S(1)} %broadcast_multiply_fusion.5) | copy-start | bytes 6148
  18.1 146.7 %copy-start.34 = (f32[4,128]{1,0:T(4,128)}, f32[4,128]{1,0:T(4,128)S(1)}, u32[]{:S(2)}) copy-start(f32[4,128]{1,0:T(4,128)S(1)} %add_rsqrt_fusion.1) | copy-start | bytes 6148
  168.4 0.7 copy-start.12
  168.4 1.2 copy-start.10
  168.4 1.2 copy-start.17
  168.8 1.0 copy-start.1
  168.8 1.0 copy-start.28
  169.3 0.6 copy-start.31
  169.3 1.2 copy-start.5
  169.8 0.7 copy-start.16
  172.8 2.2 copy-start.37
  172.8 89.7 %all-gather.15.cloned.1.call-start = ((), (), s32[]{:S(2)}) async-start(), calls=%async_computation.14 | async-start | bytes 2985984 | tf_op jit(solution)/shard_map/all_gather | solution.py:82
  174.7 105.9 %all-gather.13.cloned.1.call-start = ((), (), s32[]{:S(2)}) async-start(), calls=%async_computation.13 | async-start | bytes 1474560 | tf_op jit(solution)/shard_map/all_gather | solution.py:45
  204.6 2.3 copy-start.25
  204.6 2.3 copy-start.30
  206.0 0.8 copy-start.3
  207.8 186.9 %reduce-scatter.29.cloned.1.call-start = ((), (), s32[]{:S(2)}) async-start(), calls=%async_computation.25 | async-start | bytes 5971968 | tf_op jit(solution)/shard_map/reduce_scatter | solution.py:235
  280.6 5.5 copy-start.8
  280.6 5.5 copy-start.29
  284.7 1.4 copy-start.43
  290.4 162.7 %all-gather.17.cloned.1.call-start = ((), (), s32[]{:S(2)}) async-start(), calls=%async_computation.15 | async-start | bytes 2985984 | tf_op jit(solution)/shard_map/all_gather | solution.py:83
  398.2 97.0 %reduce-scatter.19.cloned.1.call-start = ((), (), s32[]{:S(2)}) async-start(), calls=%async_computation.18 | async-start | bytes 2949120 | tf_op jit(solution)/shard_map/reduce_scatter | solution.py:41
  453.1 6.8 copy-start.42
  458.9 1.0 copy-start.44
  463.3 67.6 %reduce-scatter.17.cloned.1.call-start = ((), (), s32[]{:S(2)}) async-start(), calls=%async_computation.16 | async-start | bytes 2949120 | tf_op jit(solution)/shard_map/reduce_scatter | solution.py:41
  469.7 83.9 %all-gather.21.cloned.1.call-start = ((), (), s32[]{:S(2)}) async-start(), calls=%async_computation.19 | async-start | bytes 1474560 | tf_op jit(solution)/shard_map/all_gather | solution.py:45
  530.9 4.3 copy-start.26
  534.4 0.8 copy-start.6
  536.0 59.6 %reduce-scatter.21.cloned.1.call-start = ((), (), s32[]{:S(2)}) async-start(), calls=%async_computation.20 | async-start | bytes 2949120 | tf_op jit(solution)/shard_map/reduce_scatter | solution.py:41
  553.6 2.2 copy-start.2
  553.6 2.2 copy-start.18
  555.9 1.0 copy-start.13
  556.3 1.0 copy-start.11
  556.9 2.1 copy-start.41
  557.3 1.0 copy-start.23
  557.8 0.7 copy-start.24
  558.3 0.7 copy-start.22
  562.4 87.2 %reduce-scatter.31.cloned.1.call-start = ((), (), s32[]{:S(2)}) async-start(), calls=%async_computation.26 | async-start | bytes 737280
  612.2 74.7 %all-gather.19.cloned.1.call-start = ((), (), s32[]{:S(2)}) async-start(), calls=%async_computation.17 | async-start | bytes 1474560 | tf_op jit(solution)/shard_map/all_gather | solution.py:45
  612.9 232.7 %reduce-scatter.25.cloned.1.call-start = ((), (), s32[]{:S(2)}) async-start(), calls=%async_computation.23 | async-start | bytes 1990656 | tf_op jit(solution)/shard_map/reduce_scatter | solution.py:233
  616.4 231.3 %reduce-scatter.27.cloned.1.call-start = ((), (), s32[]{:S(2)}) async-start(), calls=%async_computation.24 | async-start | bytes 5971968 | tf_op jit(solution)/shard_map/reduce_scatter | solution.py:234
  622.3 0.6 copy-start.33
  622.3 0.6 copy-start.35
  622.3 0.6 copy-start.38
  622.3 299.6 %reduce-scatter.33.cloned.1.call-start = ((), (), s32[]{:S(2)}) async-start(), calls=%async_computation.27 | async-start | bytes 4644864
  645.2 2.2 copy-start.7
  645.2 2.2 copy-start.15
  645.2 6.0 copy-start.27
  645.2 302.0 %all-gather.23.cloned.1.call-start = ((), (), s32[]{:S(2)}) async-start(), calls=%async_computation.21 | async-start | bytes 2949120 | tf_op jit(solution)/shard_map/all_gather | solution.py:210
  649.6 481.1 %reduce-scatter.23.cloned.1.call-start = ((), (), s32[]{:S(2)}) async-start(), calls=%async_computation.22 | async-start | bytes 11943936 | tf_op jit(solution)/shard_map/reduce_scatter | solution.py:231
  656.9 1.5 copy-start.40
  682.5 2.7 copy-start.4
  766.9 78.8 %copy-start.20 = (f32[288,144]{0,1:T(8,128)S(1)}, f32[288,144]{0,1:T(8,128)}, u32[]{:S(2)}) copy-start(f32[288,144]{0,1:T(8,128)} %param.33) | copy-start | bytes 497668
  930.2 4.9 copy-start.9
Sparse Core Ops, SparseCore 0:
  10.9 97.7 all-gather.8
  111.5 53.2 all-gather.10
  172.9 31.5 reduce-scatter.14
  207.4 55.0 all-gather.14
  264.5 16.0 all-gather.12
  290.5 104.1 reduce-scatter.28
  398.3 54.7 all-gather.16
  463.4 31.6 reduce-scatter.18
  497.8 33.0 reduce-scatter.16
  536.1 17.4 all-gather.20
  562.5 33.0 reduce-scatter.20
  612.3 22.0 reduce-scatter.30
  636.6 17.4 all-gather.18
  657.8 66.3 reduce-scatter.24
  727.6 102.9 reduce-scatter.26
  834.5 87.4 reduce-scatter.32
  923.3 23.8 all-gather.22
  950.6 179.9 reduce-scatter.22
where the time goes:
time: 1160 us; the launch traced here: 1140 us
  waiting for transfers between devices  493 us (42%)
  local copies, waits for them, and re-layouts  442 us (38%)
  blocking collectives  67.2 us (6%)
  matrix products  65 us (6%)
  other arithmetic  57.6 us (5%)
  between operations  15.7 us (1%)
    scatter x4, local copies, waits for them, and re-layouts, place_rows(): blank.at[batch, kept_index].set(kept_rows).at[batch, skip_index]  317 us
    reduce_scatter x4, waiting for transfers between devices, share_rows(): return lax.psum_scatter(values, 'mp', scatter_dimension=1, tiled=True)  110 us
    reduce_scatter x1, waiting for transfers between devices, per_device(): lax.psum_scatter(fc2_grad, 'dp', scatter_dimension=1, tiled=True)  104 us
    unnamed x111, local copies, waits for them, and re-layouts  61.3 us
    unnamed x20, waiting for transfers between devices  56.1 us
    all_gather x1, waiting for transfers between devices, per_device(): lax.all_gather(fc2_low, 'dp', axis=1, tiled=True)  54.9 us
    all_gather x1, waiting for transfers between devices, per_device(): lax.all_gather(ada_low, 'dp', axis=0, tiled=True)  51.9 us
    all_gather x1, blocking collectives, per_device(): lax.all_gather(proj_low, 'dp', axis=1, tiled=True)  38.6 us
  transfers between devices with their start and end apart: 18, of which 14 were waited for; matrix products, arithmetic and copies ran while one was open for 43% of the time, Pallas kernels for 0%

commit v1 on v0

--- a/solution.py
+++ b/solution.py
@@ -10,6 +10,18 @@
 momentum_rate = 0.9
 
 
+def doubled_up(value, axis, dim):
+    ways, here, hop = (lax.axis_size(axis), lax.axis_index(axis), value.shape[dim])
+    line, have = (value, 1)
+    while have < ways:
+        line = jnp.concatenate(
+            [line, lax.ppermute(line, axis, [(d, (d - have) % ways) for d in range(ways)])],
+            axis=dim,
+        )
+        have = 2 * have
+    return jnp.roll(line, here * hop, axis=dim)
+
+
 def layer_norm(values):
     centered = values - jnp.mean(values, axis=-1, keepdims=True)
     inverse = lax.rsqrt(jnp.mean(centered * centered, axis=-1, keepdims=True) + epsilon)
@@ -42,7 +54,7 @@
 
 
 def whole_rows(values):
-    return lax.all_gather(values, "mp", axis=1, tiled=True)
+    return doubled_up(values, "mp", 1)
 
 
 def per_device(

time: 1160 us -> 1130 us (0.974)
  waiting for transfers between devices: 493 us -> 441 us
  other arithmetic: 57.6 us -> 69.6 us
    all_gather x3 -> x0, waiting for transfers between devices: 35 us -> none  [whole_rows(): return lax.all_gather(values, 'mp', axis=1, tiled=True)]
    unnamed x20 -> x17, waiting for transfers between devices: 56.1 us -> 28.1 us
    ppermute x0 -> x6, waiting for transfers between devices: none -> 25.8 us  [doubled_up(): lax.ppermute(line, axis, [(d, (d - have) % ways) for d in range(ways)])]
    all_gather x1, waiting for transfers between devices: 32.5 us -> 18.1 us  [per_device(): lax.all_gather(fc1_low, 'dp', axis=0, tiled=True)]
    unnamed x111 -> x121, local copies, waits for them, and re-layouts: 61.3 us -> 61.6 us
  transfers between devices with their start and end apart: 18 -> 21, of which waited for: 14 -> 15; matrix products, arithmetic and copies ran while one was open for 43% -> 46% of each run, Pallas kernels for 0% -> 0%
where the time goes in v1:
time: 1130 us; the launch traced here: 1110 us
  local copies, waits for them, and re-layouts  443 us (39%)
  waiting for transfers between devices  441 us (39%)
  other arithmetic  69.6 us (6%)
  blocking collectives  67.3 us (6%)
  matrix products  63.3 us (6%)
  between operations  15.7 us (1%)
    scatter x4, local copies, waits for them, and re-layouts, place_rows(): blank.at[batch, kept_index].set(kept_rows).at[batch, skip_index]  317 us
    reduce_scatter x4, waiting for transfers between devices, share_rows(): return lax.psum_scatter(values, 'mp', scatter_dimension=1, tiled=True)  111 us
    reduce_scatter x1, waiting for transfers between devices, per_device(): lax.psum_scatter(fc2_grad, 'dp', scatter_dimension=1, tiled=True)  102 us
    unnamed x121, local copies, waits for them, and re-layouts  61.6 us
    all_gather x1, waiting for transfers between devices, per_device(): lax.all_gather(fc2_low, 'dp', axis=1, tiled=True)  54.5 us
    all_gather x1, waiting for transfers between devices, per_device(): lax.all_gather(ada_low, 'dp', axis=0, tiled=True)  52 us
    all_gather x1, blocking collectives, per_device(): lax.all_gather(proj_low, 'dp', axis=1, tiled=True)  38.6 us
    gather x4, local copies, waits for them, and re-layouts, pick_rows(): return jnp.take_along_axis(values, index[:, :, None], axis=1)  36 us
  transfers between devices with their start and end apart: 21, of which 15 were waited for; matrix products, arithmetic and copies ran while one was open for 46% of the time, Pallas kernels for 0%

profile of v1, /device:TPU:0, one launch (start us, length us, event | category | flops | bytes accessed | tf_op | source)
XLA Modules:
  0.0 1105.6 jit_solution(14315916173391728677)
XLA Ops:
  11.3 5.7 gather_fusion
  18.1 38.6 %all_gather.29 = bf16[288,1152]{0,1:T(8,128)(2,1)} all-gather(bf16[288,144]{0,1:T(8,128)(2,1)S(1)} %copy-done.24), channel_id=1, replica_groups=mesh['dp'=8,'mp'=4] {'dp'}, dimensions={1}, use_global_device_ids=true | all-gather | bytes 746496 | tf_op jit(solution)/shard_map/all_gather | solution.py:93
  56.7 52.0 %all-gather.6.cloned.1.call-done = bf16[1152,6,288]{2,0,1:T(8,128)(2,1)} async-done(((bf16[144,6,288]{2,0,1:T(8,128)(2,1)}), bf16[1152,6,288]{2,0,1:T(8,128)(2,1)}) %all-gather.6.cloned.1.call-update) | async-done | bytes 3981328 | tf_op jit(solution)/shard_map/all_gather | solution.py:91
  108.7 3.9 fusion.65
  114.4 17.3 %all_gather.27 = f32[4,6,1152]{1,0,2:T(4,128)S(1)} all-gather(f32[4,6,288]{1,0,2:T(4,128)} %copy.123), channel_id=1, replica_groups=mesh['dp'=8,'mp'=4] {'mp'}, dimensions={2}, use_global_device_ids=true | all-gather | bytes 138240 | tf_op jit(solution)/shard_map/all_gather | solution.py:111
  131.8 9.1 fusion.89
  140.9 2.7 copy.161
  143.6 2.7 copy.126
  147.7 17.1 %all-gather.8.cloned.1.call-done = bf16[3,1152,288]{2,1,0:T(8,128)(2,1)} async-done(((bf16[3,144,288]{2,1,0:T(8,128)(2,1)}), bf16[3,1152,288]{2,1,0:T(8,128)(2,1)}) %all-gather.8.cloned.1.call-update) | async-done | bytes 1990672 | tf_op jit(solution)/shard_map/all_gather | solution.py:92
  164.8 3.6 fusion.23
  177.2 2.7 copy.124
  180.0 2.8 copy.162
  182.7 2.7 copy.130
  186.8 17.8 %reduce-scatter.15.cloned.1.call-done = f32[4,32,1152]{2,1,0:T(8,128)} async-done(((f32[4,128,1152]{2,1,0:T(8,128)}), f32[4,32,1152]{2,1,0:T(8,128)}) %reduce-scatter.15.cloned.1.call-update) | async-done | bytes 589840 | tf_op jit(solution)/shard_map/reduce_scatter | solution.py:53
  207.8 4.2 convert_element_type.97
  211.9 11.0 gather_fusion.2
  226.3 4.3 subtract_multiply_fusion
  230.6 2.7 copy.128
  233.3 7.6 collective-permute-done.1
  240.9 3.5 fusion.41
  244.4 18.1 %all-gather.10.cloned.1.call-done = bf16[1152,1152]{1,0:T(8,128)(2,1)} async-done(((bf16[144,1152]{1,0:T(8,128)(2,1)}), bf16[1152,1152]{1,0:T(8,128)(2,1)}) %all-gather.10.cloned.1.call-update) | async-done | bytes 2654224 | tf_op jit(solution)/shard_map/all_gather | solution.py:94
  262.5 4.1 fusion.6
  268.0 4.2 convolution_bitcast_fusion
  273.0 102.2 %reduce-scatter.29.cloned.1.call-done = f32[1152,144]{0,1:T(8,128)} async-done(((f32[1152,1152]{0,1:T(8,128)}), f32[1152,144]{0,1:T(8,128)}) %reduce-scatter.29.cloned.1.call-update) | async-done | bytes 663568 | tf_op jit(solution)/shard_map/reduce_scatter | solution.py:247
  375.2 3.4 multiply_add_fusion.4
  379.1 54.5 %all-gather.12.cloned.1.call-done = bf16[1152,1152]{0,1:T(8,128)(2,1)} async-done(((bf16[1152,144]{0,1:T(8,128)(2,1)}), bf16[1152,1152]{0,1:T(8,128)(2,1)}) %all-gather.12.cloned.1.call-update) | async-done | bytes 2654224 | tf_op jit(solution)/shard_map/all_gather | solution.py:95
  433.6 5.8 fusion.17
  440.4 3.4 fusion.4
  443.9 6.1 fusion.2
  450.0 25.6 %reduce-scatter.19.cloned.1.call-done = f32[4,32,1152]{2,1,0:T(8,128)} async-done(((f32[4,128,1152]{2,1,0:T(8,128)}), f32[4,32,1152]{2,1,0:T(8,128)}) %reduce-scatter.19.cloned.1.call-update) | async-done | bytes 589840 | tf_op jit(solution)/shard_map/reduce_scatter | solution.py:53
  478.4 33.0 %reduce-scatter.17.cloned.1.call-done = f32[4,32,1152]{2,1,0:T(8,128)} async-done(((f32[4,128,1152]{2,1,0:T(8,128)}), f32[4,32,1152]{2,1,0:T(8,128)}) %reduce-scatter.17.cloned.1.call-update) | async-done | bytes 589840 | tf_op jit(solution)/shard_map/reduce_scatter | solution.py:53
  511.4 3.5 multiply_reduce_fusion.4
  515.2 4.2 collective-permute-done.4
  521.0 14.0 %collective-permute-done.5 = bf16[4,64,1152]{2,1,0:T(8,128)(2,1)S(1)} collective-permute-done((bf16[4,64,1152]{2,1,0:T(8,128)(2,1)S(1)}, bf16[4,64,1152]{2,1,0:T(8,128)(2,1)S(1)}, u32[]{:S(2)}, u32[]{:S(2)}) %collective-permute-start.5) | collective-permute-done | bytes 589856 | tf_op jit(solution)/shard_map/ppermute | solution.py:18
  540.2 3.4 convolution_bitcast_fusion.3
  543.7 34.7 %reduce-scatter.21.cloned.1.call-done = f32[4,32,1152]{2,1,0:T(8,128)} async-done(((f32[4,128,1152]{2,1,0:T(8,128)}), f32[4,32,1152]{2,1,0:T(8,128)}) %reduce-scatter.21.cloned.1.call-update) | async-done | bytes 589840 | tf_op jit(solution)/shard_map/reduce_scatter | solution.py:53
  587.0 3.8 copy.157
  590.8 4.1 reshape.212
  595.0 3.4 convolution_bitcast_fusion.4
  598.5 5.7 convolution_bitcast_fusion.1
  604.9 4.7 convolution_bitcast_fusion.2
  609.6 8.6 copy.159
  618.2 9.0 reshape.214
  633.3 5.7 fusion.61
  639.9 11.0 gather_fusion.3
  653.3 3.4 broadcast_select_fusion
  658.2 8.4 gather_fusion.1
  671.2 2.5 broadcast_select_fusion.2
  673.7 3.5 fusion.36
  678.8 78.5 %scatter_fusion = bf16[4,256,1152]{2,1,0:T(8,128)(2,1)} fusion(bf16[4,256,1152]{2,1,0:T(8,128)(2,1)} %broadcast_in_dim.28, s32[512]{0:T(512)S(1)} %get-tuple-element.153, bf16[512,1152]{1,0:T(8,128)(2,1)} %bitcast.188), kind=kCustom, calls=%fused_computation.4 | custom fusion | bytes 3543040 | tf_op jit(solution)/shard_map/scatter | solution.py:49
  757.2 78.7 %scatter_fusion.1 = bf16[4,256,1152]{2,1,0:T(8,128)(2,1)} fusion(bf16[4,256,1152]{2,1,0:T(8,128)(2,1)} %scatter_fusion, s32[512]{0:T(512)S(1)} %get-tuple-element.151, bf16[512,1152]{1,0:T(8,128)(2,1)} %bitcast.187), kind=kCustom, calls=%fused_computation.5 | custom fusion | bytes 3543040 | tf_op jit(solution)/shard_map/scatter | solution.py:49
  838.0 4.0 convolution_bitcast_fusion.5
  842.1 11.3 %psum.7 = f32[4,1152]{1,0:T(4,128)S(1)} all-reduce(f32[4,1152]{1,0:T(4,128)S(1)} %convolution_bitcast_fusion.5), channel_id=1, replica_groups=mesh['dp'=8,'mp'=4] {'mp'}, use_global_device_ids=true, to_apply=%region_26.30 | all-reduce | flops 4608 | bytes 36864 | tf_op jit(solution)/shard_map/psum | solution.py:237
  854.1 3.1 multiply_add_fusion.5
  857.2 27.9 %reduce-scatter.33.cloned.1.call-done = f32[144,864]{1,0:T(8,128)} async-done(((f32[1152,864]{1,0:T(8,128)}), f32[144,864]{1,0:T(8,128)}) %reduce-scatter.33.cloned.1.call-update) | async-done | bytes 497680
  887.4 2.4 copy.160
  889.9 3.5 multiply_add_fusion.2
  893.3 2.5 copy.144
  899.4 10.9 all-gather.14.cloned.1.call-done
  910.3 2.5 broadcast_in_dim.35
  912.8 80.1 %scatter_fusion.2 = f32[4,256,1152]{2,1,0:T(8,128)} fusion(f32[4,256,1152]{2,1,0:T(8,128)} %broadcast_in_dim.35, s32[512]{0:T(512)S(1)} %get-tuple-element.153, f32[512,1152]{1,0:T(8,128)} %bitcast.197), kind=kCustom, calls=%fused_computation.6 | custom fusion | bytes 7081984 | tf_op jit(solution)/shard_map/scatter | solution.py:49
  992.9 79.7 %scatter_fusion.3 = f32[4,256,1152]{2,1,0:T(8,128)} fusion(f32[4,256,1152]{2,1,0:T(8,128)} %scatter_fusion.2, s32[512]{0:T(512)S(1)} %get-tuple-element.151, f32[512,1152]{1,0:T(8,128)} %bitcast.184), kind=kCustom, calls=%fused_computation.7 | custom fusion | bytes 7081984 | tf_op jit(solution)/shard_map/scatter | solution.py:49
  1072.6 21.2 %reduce-scatter.23.cloned.1.call-done = f32[144,6,288]{2,0,1:T(8,128)} async-done(((f32[1152,6,288]{2,0,1:T(8,128)}), f32[144,6,288]{2,0,1:T(8,128)}) %reduce-scatter.23.cloned.1.call-update) | async-done | bytes 995344 | tf_op jit(solution)/shard_map/reduce_scatter | solution.py:243
  1093.8 4.8 multiply_add_fusion
  (204 shorter events, 73.0 us)
Async XLA Ops:
  7.2 4.1 copy-start
  7.2 2.5 copy-start.16
  7.2 3.4 copy-start.22
  7.2 4.0 copy-start.44
  7.2 101.4 %all-gather.6.cloned.1.call-start = ((), (), s32[]{:S(2)}) async-start(), calls=%async_computation.10 | async-start | bytes 5971968 | tf_op jit(solution)/shard_map/all_gather | solution.py:91
  9.7 155.1 %all-gather.8.cloned.1.call-start = ((), (), s32[]{:S(2)}) async-start(), calls=%async_computation.11 | async-start | bytes 2985984 | tf_op jit(solution)/shard_map/all_gather | solution.py:92
  10.5 194.0 %reduce-scatter.15.cloned.1.call-start = ((), (), s32[]{:S(2)}) async-start(), calls=%async_computation.12 | async-start | bytes 2949120 | tf_op jit(solution)/shard_map/reduce_scatter | solution.py:53
  17.0 1.1 copy-start.24
  17.5 147.2 %copy-start.38 = (f32[4,128]{1,0:T(4,128)}, f32[4,128]{1,0:T(4,128)S(1)}, u32[]{:S(2)}) copy-start(f32[4,128]{1,0:T(4,128)S(1)} %broadcast_multiply_fusion.5) | copy-start | bytes 6148
  18.1 146.7 %copy-start.40 = (f32[4,128]{1,0:T(4,128)}, f32[4,128]{1,0:T(4,128)S(1)}, u32[]{:S(2)}) copy-start(f32[4,128]{1,0:T(4,128)S(1)} %add_rsqrt_fusion.1) | copy-start | bytes 6148
  168.4 0.7 copy-start.14
  168.4 1.3 copy-start.12
  168.4 1.3 copy-start.20
  168.8 1.0 copy-start.1
  169.3 1.2 copy-start.5
  172.8 89.7 %all-gather.10.cloned.1.call-start = ((), (), s32[]{:S(2)}) async-start(), calls=%async_computation.13 | async-start | bytes 2985984 | tf_op jit(solution)/shard_map/all_gather | solution.py:94
  174.8 200.4 %reduce-scatter.29.cloned.1.call-start = ((), (), s32[]{:S(2)}) async-start(), calls=%async_computation.22 | async-start | bytes 5971968 | tf_op jit(solution)/shard_map/reduce_scatter | solution.py:247
  204.6 2.3 copy-start.28
  204.6 2.3 copy-start.32
  206.0 0.8 copy-start.3
  206.0 1.7 copy-start.33
  206.3 1.5 copy-start.35
  207.8 15.2 %collective-permute-start = (bf16[4,32,1152]{2,1,0:T(8,128)(2,1)}, bf16[4,32,1152]{2,1,0:T(8,128)(2,1)}, u32[]{:S(2)}, u32[]{:S(2)}) collective-permute-start(bf16[4,32,1152]{2,1,0:T(8,128)(2,1)} %add_convert_fusion.2), channel_id=1, source_target_pairs={{0,3},{1,0},{2,1},{3,2},{4,7},{5,4},{6,5},{7,6},{8,11},{9,8},{10,9... | collective-permute-start | bytes 884744 | tf_op jit(solution)/shard_map/ppermute | solution.py:18
  224.9 16.1 %collective-permute-start.1 = (bf16[4,64,1152]{2,1,0:T(8,128)(2,1)}, bf16[4,64,1152]{2,1,0:T(8,128)(2,1)}, u32[]{:S(2)}, u32[]{:S(2)}) collective-permute-start(bf16[4,64,1152]{2,1,0:T(8,128)(2,1)} %pad_maximum_fusion.1), channel_id=1, source_target_pairs={{0,2},{1,3},{2,0},{3,1},{4,6},{5,7},{6,4},{7,5},{8,10},{9,11},{10,... | collective-permute-start | bytes 1769480 | tf_op jit(solution)/shard_map/ppermute | solution.py:18
  262.5 5.5 copy-start.9
  262.5 5.5 copy-start.31
  266.6 1.4 copy-start.48
  272.3 161.3 %all-gather.12.cloned.1.call-start = ((), (), s32[]{:S(2)}) async-start(), calls=%async_computation.14 | async-start | bytes 2985984 | tf_op jit(solution)/shard_map/all_gather | solution.py:95
  378.6 96.9 %reduce-scatter.19.cloned.1.call-start = ((), (), s32[]{:S(2)}) async-start(), calls=%async_computation.16 | async-start | bytes 2949120 | tf_op jit(solution)/shard_map/reduce_scatter | solution.py:53
  433.6 6.8 copy-start.47
  439.4 1.0 copy-start.49
  443.8 67.6 %reduce-scatter.17.cloned.1.call-start = ((), (), s32[]{:S(2)}) async-start(), calls=%async_computation.15 | async-start | bytes 2949120 | tf_op jit(solution)/shard_map/reduce_scatter | solution.py:53
  449.9 25.6 %copy-start.34 = (f32[4,32]{1,0:T(4,128)S(1)}, f32[4,32]{1,0:T(4,128)}, u32[]{:S(2)}) copy-start(f32[4,32]{1,0:T(4,128)} %copy-done.33) | copy-start | bytes 1540
  450.0 128.4 %reduce-scatter.21.cloned.1.call-start = ((), (), s32[]{:S(2)}) async-start(), calls=%async_computation.17 | async-start | bytes 2949120 | tf_op jit(solution)/shard_map/reduce_scatter | solution.py:53
  511.4 3.5 copy-start.29
  511.4 9.6 copy-start.37
  514.9 6.1 copy-start.7
  514.9 21.6 %copy-start.6 = (bf16[288,1152]{0,1:T(8,128)(2,1)S(1)}, bf16[288,1152]{0,1:T(8,128)(2,1)}, u32[]{:S(2)}) copy-start(bf16[288,1152]{0,1:T(8,128)(2,1)} %all_gather.29) | copy-start | bytes 1990660
  514.9 4.5 collective-permute-start.4
  519.4 15.5 %collective-permute-start.5 = (bf16[4,64,1152]{2,1,0:T(8,128)(2,1)S(1)}, bf16[4,64,1152]{2,1,0:T(8,128)(2,1)S(1)}, u32[]{:S(2)}, u32[]{:S(2)}) collective-permute-start(bf16[4,64,1152]{2,1,0:T(8,128)(2,1)S(1)} %pad_maximum_fusion.3), channel_id=1, source_target_pairs={{0,2},{1,3},{2,0},{3,1},{4,6},{5,7},{6,4},{7,5},{8,10},{9,11},{10,... | collective-permute-start | bytes 1769480 | tf_op jit(solution)/shard_map/ppermute | solution.py:18
  521.0 16.1 %copy-start.2 = (f32[4,4,128,128]{2,3,1,0:T(8,128)S(1)}, f32[4,4,128,128]{2,3,1,0:T(8,128)}, u32[]{:S(2)}) copy-start(f32[4,4,128,128]{2,3,1,0:T(8,128)} %copy-done.1) | copy-start | bytes 3145732
  521.0 16.1 %copy-start.21 = (bf16[1,4,128,288]{2,3,0,1:T(8,128)(2,1)S(1)}, bf16[1,4,128,288]{2,3,0,1:T(8,128)(2,1)}, u32[]{:S(2)}) copy-start(bf16[1,4,128,288]{2,3,0,1:T(8,128)(2,1)} %copy-done.20) | copy-start | bytes 884740
  536.4 1.1 copy-start.4
  537.1 1.0 copy-start.15
  537.5 1.0 copy-start.13
  538.0 2.2 copy-start.46
  538.5 1.0 copy-start.26
  539.5 0.7 copy-start.25
  543.6 88.0 %reduce-scatter.31.cloned.1.call-start = ((), (), s32[]{:S(2)}) async-start(), calls=%async_computation.23 | async-start | bytes 737280
  595.0 241.0 %reduce-scatter.25.cloned.1.call-start = ((), (), s32[]{:S(2)}) async-start(), calls=%async_computation.20 | async-start | bytes 1990656 | tf_op jit(solution)/shard_map/reduce_scatter | solution.py:245
  598.5 255.6 %reduce-scatter.27.cloned.1.call-start = ((), (), s32[]{:S(2)}) async-start(), calls=%async_computation.21 | async-start | bytes 5971968 | tf_op jit(solution)/shard_map/reduce_scatter | solution.py:246
  604.2 280.8 %reduce-scatter.33.cloned.1.call-start = ((), (), s32[]{:S(2)}) async-start(), calls=%async_computation.24 | async-start | bytes 4644864
  627.1 2.3 copy-start.8
  627.1 2.3 copy-start.17
  627.2 6.1 copy-start.30
  627.2 283.1 %all-gather.14.cloned.1.call-start = ((), (), s32[]{:S(2)}) async-start(), calls=%async_computation.18 | async-start | bytes 2949120 | tf_op jit(solution)/shard_map/all_gather | solution.py:222
  631.6 462.2 %reduce-scatter.23.cloned.1.call-start = ((), (), s32[]{:S(2)}) async-start(), calls=%async_computation.19 | async-start | bytes 11943936 | tf_op jit(solution)/shard_map/reduce_scatter | solution.py:243
  639.0 1.0 copy-start.11
  639.0 1.0 copy-start.45
  639.9 11.0 collective-permute-start.2
  650.9 2.4 copy-start.19
  651.8 21.9 %collective-permute-start.3 = (bf16[4,64,1152]{2,1,0:T(8,128)(2,1)}, bf16[4,64,1152]{2,1,0:T(8,128)(2,1)}, u32[]{:S(2)}, u32[]{:S(2)}) collective-permute-start(bf16[4,64,1152]{2,1,0:T(8,128)(2,1)} %pad_maximum_fusion.2), channel_id=1, source_target_pairs={{0,2},{1,3},{2,0},{3,1},{4,6},{5,7},{6,4},{7,5},{8,10},{9,11},{10,... | collective-permute-start | bytes 1769480 | tf_op jit(solution)/shard_map/ppermute | solution.py:18
  757.2 78.7 %copy-start.23 = (f32[288,144]{0,1:T(8,128)S(1)}, f32[288,144]{0,1:T(8,128)}, u32[]{:S(2)}) copy-start(f32[288,144]{0,1:T(8,128)} %param.35) | copy-start | bytes 497668
  893.3 4.9 copy-start.10
  (7 other events, 4.6 us)
Sparse Core Ops, SparseCore 0:
  10.9 97.7 all-gather.5
  111.5 53.2 all-gather.7
  172.9 31.5 reduce-scatter.14
  207.4 55.0 all-gather.9
  272.4 102.7 reduce-scatter.28
  378.8 54.7 all-gather.11
  443.9 31.6 reduce-scatter.18
  478.3 33.0 reduce-scatter.16
  543.7 34.5 reduce-scatter.20
  595.1 22.0 reduce-scatter.30
  621.1 66.1 reduce-scatter.24
  690.7 102.8 reduce-scatter.26
  797.6 87.3 reduce-scatter.32
  886.5 23.8 all-gather.13
  913.8 179.9 reduce-scatter.22
